TPU v7x, 256 devices: a whole 4x4x8 slice. The times are simulated.
256 devices in a mesh: req: 32 (over z, y), seq: 8 (over x, core).
Axes of the slice: x: 4, y: 4, z: 8, core: 2. Of those that a mesh axis runs over, the one named last changes fastest.
Arguments:
- tokens: bfloat16 [32, 4096, 2560], P('req', 'seq'), may hold values from -6 to 6
- mix_weight: bfloat16 [2560, 2816], P(('req', 'seq')), may hold values from -0.125 to 0.125
- step_weight: bfloat16 [2560, 40], P(('req', 'seq')), may hold values from -0.125 to 0.125
- conv_weight: float32 [4, 2816], replicated, may hold values from -3 to 3
- conv_bias: float32 [2816], replicated, may hold values from -3 to 3
- step_bias: float32 [40], replicated, may hold values from -5 to -3
- decay_rate: float32 [40], replicated, may hold values from 0.00048828125 to 1
- skip_gain: float32 [40], replicated, may hold values from 0.5 to 2
- norm_gain: float32 [2560], replicated, may hold values from 0.1 to 1.9
- prompt_len: int32 [32], replicated, may hold values from 1024 to 4096, as said below
- prompt_start: int32 [32], replicated, may hold values from 0 to 3072, as said below
- deal: int32 [32], replicated, may hold values from 0 to 31, as said below
Outputs:
- result: bfloat16 [32, 4096, 2560], P('req', 'seq')
- final_state: float32 [32, 40, 64, 128], P('req', 'seq')
Inputs may be any that keep to these rules, and one draw needn't show every extreme that they name: `prompt_len`: one prompt has exactly 4096 positions and one exactly a quarter of 4096. prompt_start plus prompt_len is at most 4096 for every request. `deal`: a permutation of the requests; some slot s holds request (s + 16) modulo 32.
All inputs are finite; a program needn't handle non-finite values.
Results may differ from a plain program's by a relative error of at most 0.0035.
Values may be sent and summed in bfloat16 or wider, within the bound.
A program may use at most 128 MiB of HBM per device.

v0:
```python
import jax
import jax.numpy as jnp
from jax import lax
from jax.sharding import PartitionSpec as P

GROUP = 256
EPS = 1e-05


def passed_along(block, axis, distance):
    devices = range(lax.axis_size(axis))
    route = [(i - distance, i) for i in devices if i - distance in devices]
    return lax.ppermute(block, axis, route)


def carried_in(part, axis, combine, identity):
    place = lax.axis_index(axis)
    gathered = jax.tree.map(lambda a: lax.all_gather(a, axis), part)
    state = jax.tree.map(lambda a, e: jnp.zeros_like(a) + jnp.asarray(e, a.dtype), part, identity)

    def one(step, state):
        return combine(
            state, jax.tree.map(lambda a: lax.dynamic_index_in_dim(a, step, 0, False), gathered)
        )

    return lax.fori_loop(0, place, one, state)


def broadcast(x, axis, root):
    mine = lax.axis_index(axis) == root
    return lax.psum(jnp.where(mine, x, jnp.zeros_like(x)), axis)


def on_device(
    tokens,
    mix_weight,
    step_weight,
    conv_weight,
    conv_bias,
    step_bias,
    decay_rate,
    skip_gain,
    norm_gain,
    prompt_len,
    prompt_start,
    deal,
):
    seq_count = lax.axis_size("seq")
    seq_index = lax.axis_index("seq")
    req_index = lax.axis_index("req")
    rows = tokens[0]
    span = rows.shape[0]
    total_reqs = deal.shape[0]
    slots = jnp.arange(total_reqs, dtype=jnp.int32)
    request = jnp.sum(jnp.where(slots == req_index, deal, 0))
    length = jnp.sum(jnp.where(slots == request, prompt_len, 0))
    start = jnp.sum(jnp.where(slots == request, prompt_start, 0))
    place = seq_index * span + jnp.arange(span, dtype=jnp.int32)
    valid = ((place >= start) & (place < start + length)).astype(jnp.float32)
    whole_mix, whole_step = (
        lax.all_gather(mix_weight, ("req", "seq"), axis=0, tiled=True),
        lax.all_gather(step_weight, ("req", "seq"), axis=0, tiled=True),
    )
    mixed = jnp.dot(rows, whole_mix, preferred_element_type=jnp.float32)
    raw_step = jnp.dot(rows, whole_step, preferred_element_type=jnp.float32)
    mixed = (mixed * valid[:, None]).astype(jnp.bfloat16)
    taps = conv_weight.shape[0]
    edge = passed_along(mixed[span - (taps - 1) :], "seq", 1)
    padded = jnp.concatenate([edge, mixed], axis=0)
    conv_sum = jnp.zeros(mixed.shape, jnp.float32) + conv_bias[None, :]
    for offset in range(taps):
        conv_sum = conv_sum + conv_weight[offset][None, :] * padded[offset : offset + span].astype(
            jnp.float32
        )
    convolved = jax.nn.silu(conv_sum).astype(jnp.bfloat16)
    heads = decay_rate.shape[0]
    inner = norm_gain.shape[0]
    head_dim = inner // heads
    nstate = (mixed.shape[1] - inner) // 2
    blocks = span // GROUP
    inputs = convolved[:, :inner].reshape(span, heads, head_dim)
    mixed_b = convolved[:, inner : inner + nstate]
    mixed_c = convolved[:, inner + nstate :]
    step_size = jax.nn.softplus(raw_step + step_bias[None, :]) * valid[:, None]
    pieces = (
        inputs.reshape(blocks, GROUP, heads, head_dim),
        mixed_b.reshape(blocks, GROUP, nstate),
        mixed_c.reshape(blocks, GROUP, nstate),
        step_size.reshape(blocks, GROUP, heads),
    )

    def local_group(block):
        part_in, part_b, part_c, part_step = block
        cum_decay = jnp.cumsum(-part_step * decay_rate[None, :], axis=0)
        places = jnp.arange(GROUP, dtype=jnp.int32)
        causal = places[:, None] >= places[None, :]
        spread = cum_decay[:, None, :] - cum_decay[None, :, :]
        spread = jnp.where(causal[:, :, None], spread, -1e30)
        scores = jnp.einsum("qn,kn->qk", part_c, part_b, preferred_element_type=jnp.float32)
        mixing = (jnp.exp(spread) * scores[:, :, None] * part_step[None, :, :]).astype(jnp.bfloat16)
        inner_out = jnp.einsum("qkh,khp->qhp", mixing, part_in, preferred_element_type=jnp.float32)
        to_end = jnp.exp(cum_decay[-1][None, :] - cum_decay) * part_step
        scaled = (to_end[:, :, None] * part_in.astype(jnp.float32)).astype(jnp.bfloat16)
        local = jnp.einsum("khp,kn->hpn", scaled, part_b, preferred_element_type=jnp.float32)
        return (inner_out, cum_decay, local)

    inner_out, cum_decay, group_state = lax.map(local_group, pieces)
    totals = cum_decay[:, -1, :]

    def advance(carry, item):
        group_total, group_local = item
        return (jnp.exp(group_total)[:, None, None] * carry + group_local, carry)

    dev_state, entry_zero = lax.scan(
        advance, jnp.zeros((heads, head_dim, nstate), jnp.float32), (totals, group_state)
    )
    before = jnp.cumsum(totals, axis=0) - totals
    dev_decay = jnp.exp(jnp.sum(totals, axis=0))

    def chain(earlier, later):
        return (earlier[0] * later[0], later[0][:, None, None] * earlier[1] + later[1])

    incoming_decay, incoming = carried_in(
        (dev_decay, dev_state), "seq", chain, (jnp.ones_like(dev_decay), jnp.zeros_like(dev_state))
    )
    entry = entry_zero + jnp.exp(before)[:, :, None, None] * incoming[None]
    carried = jnp.einsum(
        "cqn,chpn->cqhp", pieces[2].astype(jnp.float32), entry, precision=lax.Precision.HIGHEST
    )
    carried = carried * jnp.exp(cum_decay)[:, :, :, None]
    outputs = (inner_out + carried).reshape(span, heads, head_dim) + skip_gain[
        None, :, None
    ] * inputs.astype(jnp.float32)
    flat = outputs.reshape(span, inner)
    factor = lax.rsqrt(jnp.mean(flat * flat, axis=1, keepdims=True) + EPS)
    result = (flat * factor * norm_gain[None, :] * valid[:, None]).astype(jnp.bfloat16)[None]
    share = heads // seq_count
    leaving = dev_decay[:, None, None] * incoming + dev_state
    last_state = broadcast(leaving, "seq", seq_count - 1)
    own_state = lax.dynamic_slice_in_dim(last_state, seq_index * share, share, 0)[None]
    wanted = jnp.sum(jnp.where(deal == req_index, slots, 0))
    piece = lax.all_gather(own_state, "req", axis=0, tiled=True)
    count = piece.shape[0]
    chosen = jnp.arange(count, dtype=jnp.int32) == wanted
    final_state = jnp.zeros_like(own_state) + jnp.sum(
        jnp.where(chosen[:, None, None, None], piece, 0.0), axis=0, keepdims=True
    )
    return (result, final_state)


def solution(mesh):
    return jax.shard_map(
        on_device,
        mesh=mesh,
        in_specs=(
            P("req", "seq", None),
            P(("req", "seq"), None),
            P(("req", "seq"), None),
            P(),
            P(),
            P(),
            P(),
            P(),
            P(),
            P(),
            P(),
            P(),
        ),
        out_specs=(P("req", "seq", None), P("req", "seq", None, None)),
        check_vma=False,
    )
```

profile of v0, /device:TPU:2, one launch (start us, length us, event | category | flops | bytes accessed | tf_op | source)
XLA Modules:
  0.0 482.0 jit_solution(1051136293453293092)
XLA Ops:
  8.0 70.5 %all-gather.4 = bf16[256,10,40]{2,1,0:T(8,128)(2,1)} all-gather(bf16[1,10,40]{2,1,0:T(8,128)(2,1)} %bitcast.158), channel_id=1, replica_groups=mesh['req'=32,'seq'=8] {'req','seq'}, dimensions={0}, use_global_device_ids=true | all-gather | bytes 205600 | tf_op jit(solution)/shard_map/all_gather | solution.py:62
  88.7 60.2 %all-gather.13.cloned.1.call-done = bf16[256,10,2816]{2,1,0:T(8,128)(2,1)} async-done(((bf16[1,10,2816]{2,1,0:T(8,128)(2,1)}), bf16[256,10,2816]{2,1,0:T(8,128)(2,1)}) %all-gather.13.cloned.1.call-update) | async-done | bytes 14417936 | tf_op jit(solution)/shard_map/all_gather | solution.py:61
  149.0 25.3 %reshape.117 = bf16[2560,2816]{1,0:T(8,128)(2,1)} reshape(bf16[256,10,2816]{2,1,0:T(8,128)(2,1)} %all-gather.13.cloned.1.call-done) | data formatting | bytes 28835840
  174.2 11.5 %multiply_convert_fusion.6 = bf16[512,2816]{1,0:T(8,128)(2,1)S(1)} fusion(bf16[2560,2816]{1,0:T(8,128)(2,1)} %reshape.117, f32[512]{0:T(512)S(1)} %fusion.50, bf16[1,512,2560]{2,1,0:T(8,128)(2,1)S(1)} %copy-done), kind=kOutput, calls=%fused_computation.48 | convolution fusion | flops 7384858624 | bytes 19924992 | tf_op jit(solution)/shard_map/dot_general | solution.py:64
  187.4 2.3 collective-permute-start
  189.9 2.6 collective-permute-done
  192.5 7.8 %multiply_convert_fusion.5 = bf16[512,2816]{1,0:T(8,128)(2,1)S(1)} fusion(bf16[512,2816]{1,0:T(8,128)(2,1)} %copy-done.7, bf16[3,2816]{1,0:T(4,128)(2,1)S(1)} %collective-permute-done, f32[2816]{0:T(1024)S(1)} %get-tuple-element.187, f32[2816]{0:T(1024)S(1)} %get-tuple-element.188, f32[2816]{0:T(1024)S(1)} %get-tuple-element.186, ...), kind=kLoop, calls=%fused_computation.47 | loop fusion | flops 37486592 | bytes 5840384 | tf_op jit(solution)/shard_map/convert_element_type | solution.py:75
  203.5 7.5 %reshape.124 = bf16[2,256,40,64]{3,2,1,0:T(8,128)(2,1)} reshape(bf16[512,2560]{1,0:T(8,128)(2,1)} %slice.64) | data formatting | bytes 5242880 | tf_op jit(solution)/shard_map/reshape;reshape | solution.py:86
  211.0 6.4 %copy.40 = bf16[2,256,40,64]{1,3,2,0:T(8,128)(2,1)} copy(bf16[2,256,40,64]{3,2,1,0:T(8,128)(2,1)} %reshape.124) | data formatting | bytes 5242880 | tf_op jit(solution)/shard_map/while | solution.py:107
  219.3 17.0 %while.39 = (s32[]{:T(128)}, f32[2,256,40,64]{1,3,2,0:T(8,128)}, f32[2,256,40]{1,2,0:T(8,128)S(1)}, f32[2,40,64,128]{3,2,1,0:T(8,128)}, bf16[2,256,40,64]{1,3,2,...) while((s32[]{:T(128)}, f32[2,256,40,64]{1,3,2,0:T(8,128)}, ...), condition=%wide.region_6.7_spmd, body=%wide.region_3.6_spmd.sunk | while | flops 536604800 | bytes 18677688 | solution.py:107
  220.5 5.3 %bitcast_dynamic-update-slice_fusion.4 = f32[2,256,40,64]{1,3,2,0:T(8,128)} fusion(f32[2,256,40,64]{1,3,2,0:T(8,128)} %get-tuple-element.363, s32[]{:T(128)} %get-tuple-element.362, f32[256,40]{0,1:T(8,128)S(1)} %bitcast.155, f32[256,256]{1,0:T(8,128)S(1)} %fusion.74, f32[256,40]{0,1:T(8,128)S(1)} %bitcast_bitcast_fusion.3, ...), kind=kOutput, calls=%fused_computation.15.clone.1 | convolution fusion | flops 348651520 | bytes 4383744 | tf_op jit(solution)/shard_map/while/body/eval_jaxpr/qkh,khp->qhp/dot_general | solution.py:101
  229.0 5.3 %bitcast_dynamic-update-slice_fusion.4 = f32[2,256,40,64]{1,3,2,0:T(8,128)} fusion(f32[2,256,40,64]{1,3,2,0:T(8,128)} %get-tuple-element.363, s32[]{:T(128)} %get-tuple-element.362, f32[256,40]{0,1:T(8,128)S(1)} %bitcast.155, f32[256,256]{1,0:T(8,128)S(1)} %fusion.74, f32[256,40]{0,1:T(8,128)S(1)} %bitcast_bitcast_fusion.3, ...), kind=kOutput, calls=%fused_computation.15.clone.1 | convolution fusion | flops 348651520 | bytes 4383744 | tf_op jit(solution)/shard_map/while/body/eval_jaxpr/qkh,khp->qhp/dot_general | solution.py:101
  238.3 5.6 %while.41 = (s32[]{:T(128)}, f32[40,64,128]{2,1,0:T(8,128)S(1)}, f32[2,40,64,128]{3,2,1,0:T(8,128)}, f32[2,40]{1,0:T(2,128)S(1)}, f32[2,40,64,128]{3,2,1,0:T(8,128)}, /*index=5*/s32[]{:T(128)}, s32[]{:T(128)}) while((s32[]{:T(128)}, f32[40,64,128]{2,1,0:T(8,128)S(1)}, f32[2,40,64,128]{3,2,1,0:T(8,128)}, f32[2,40]{1,0:T(2,128)S(1)}, ...), condition=%wide.region_8.9_spmd.clone, body=%wide.region_7.8_spmd.clone.sunk | while | flops 1310723 | bytes 6554688 | solution.py:114
  246.6 10.0 %all-reduce = f32[320]{0:T(512)S(1)} all-reduce(f32[320]{0:T(512)S(1)} %get-tuple-element.232), channel_id=2, replica_groups=mesh['req'=32,'seq'=8] {'seq'}, use_global_device_ids=true, to_apply=%add | all-reduce | flops 320 | bytes 2560
  256.6 46.0 %all-gather.9.cloned.1.call-done = f32[320,64,128]{2,1,0:T(8,128)} async-done(((f32[40,64,128]{2,1,0:T(8,128)}), f32[320,64,128]{2,1,0:T(8,128)}) %all-gather.9.cloned.1.call-update) | async-done | bytes 10485776 | tf_op jit(solution)/shard_map/all_gather | solution.py:18
  302.8 3.3 while.40
  307.7 74.1 %all-reduce.3.cloned.1.call-done = f32[40,64,128]{2,1,0:T(8,128)} async-done(((f32[40,64,128]{2,1,0:T(8,128)}), f32[40,64,128]{2,1,0:T(8,128)}) %all-reduce.3.cloned.1.call-update) | async-done | bytes 1310736 | tf_op jit(solution)/shard_map/psum | solution.py:31
  384.3 8.0 %multiply_add_fusion.1 = f32[2,256,40,64]{1,3,2,0:T(8,128)} fusion(f32[2,256,40,64]{1,3,2,0:T(8,128)} %get-tuple-element.123, f32[2,256,40]{1,2,0:T(8,128)S(1)} %exp.56, bf16[2,256,128,1]{2,1,3,0:T(8,128)(2,1)S(1)} %bitcast.154, f32[2,40,64,128]{3,2,1,0:T(8,128)} %get-tuple-element.126, f32[40,64,128]{2,1,0:T(8,128)S(1)} %get-tuple-element.128, ...), kind=kOutput, calls=%fused_computation.53 | convolution fusion | flops 2017198080 | bytes 14631232 | tf_op jit(solution)/shard_map/cqn,chpn->cqhp/dot_general | solution.py:127
  392.4 8.6 %copy.47 = f32[2,256,40,64]{3,2,1,0:T(8,128)} copy(f32[2,256,40,64]{1,3,2,0:T(8,128)} %multiply_add_fusion.1) | data formatting | bytes 10485760 | tf_op jit(solution)/shard_map/reshape | solution.py:131
  401.0 9.6 %reshape.125 = f32[512,2560]{1,0:T(8,128)} reshape(f32[2,256,40,64]{3,2,1,0:T(8,128)} %copy.47) | data formatting | bytes 10485760 | tf_op jit(solution)/shard_map/reshape | solution.py:131
  410.6 4.4 multiply_reduce_fusion
  415.4 4.7 fusion.30
  420.1 51.5 %all-gather.11.cloned.1.call-done = f32[160,64,128]{2,1,0:T(8,128)} async-done(((f32[5,64,128]{2,1,0:T(8,128)}), f32[160,64,128]{2,1,0:T(8,128)}) %all-gather.11.cloned.1.call-update) | async-done | bytes 5242896 | tf_op jit(solution)/shard_map/all_gather | solution.py:142
  471.6 3.9 select_reduce_fusion
  (107 shorter events, 40.3 us)
Async XLA Ops:
  7.2 80.0 %copy-start = (bf16[1,512,2560]{2,1,0:T(8,128)(2,1)S(1)}, bf16[1,512,2560]{2,1,0:T(8,128)(2,1)}, u32[]{:S(2)}) copy-start(bf16[1,512,2560]{2,1,0:T(8,128)(2,1)} %param.18) | copy-start | bytes 7864324
  7.2 141.8 %all-gather.13.cloned.1.call-start = ((), (), s32[]{:S(2)}) async-start(), calls=%async_computation.3 | async-start | bytes 23158784 | tf_op jit(solution)/shard_map/all_gather | solution.py:61
  7.9 294.7 %all-gather.9.cloned.1.call-start = ((), (), s32[]{:S(2)}) async-start(), calls=%async_computation.1 | async-start | bytes 11796480 | tf_op jit(solution)/shard_map/all_gather | solution.py:18
  174.2 15.5 %copy-start.8 = (f32[4,2816]{1,0:T(4,128)S(1)}, f32[4,2816]{1,0:T(4,128)}, u32[]{:S(2)}) copy-start(f32[4,2816]{1,0:T(4,128)} %param.21) | copy-start | bytes 135172
  174.2 18.2 %copy-start.10 = (f32[2816]{0:T(1024)S(1)}, f32[2816]{0:T(1024)}, u32[]{:S(2)}) copy-start(f32[2816]{0:T(1024)} %param.22) | copy-start | bytes 33796
  185.8 1.6 copy-start.7
  187.4 5.1 %collective-permute-start = (bf16[3,2816]{1,0:T(4,128)(2,1)S(1)}, bf16[3,2816]{1,0:T(4,128)(2,1)S(1)}, u32[]{:S(2)}, u32[]{:S(2)}) collective-permute-start(bf16[3,2816]{1,0:T(4,128)(2,1)S(1)} %slice.59), channel_id=1, source_target_pairs={{0,1},{1,2},{2,3},{3,4},{4,5},{5,6},{6,7},{8,9},{9,10},{10,11},{11... | collective-permute-start | bytes 50696 | tf_op jit(solution)/shard_map/ppermute | solution.py:13
  200.3 1.5 copy-start.5
  211.0 8.2 %copy-start.9 = (f32[40]{0:T(128)S(1)}, f32[40]{0:T(128)}, u32[]{:S(2)}) copy-start(f32[40]{0:T(128)} %param.24) | copy-start | bytes 484
  220.5 5.6 %copy-start.6 = (bf16[2,256,40,64]{1,3,2,0:T(8,128)(2,1)S(1)}, bf16[2,256,40,64]{1,3,2,0:T(8,128)(2,1)}, u32[]{:S(2)}) copy-start(bf16[2,256,40,64]{1,3,2,0:T(8,128)(2,1)} %get-tuple-element.377) | copy-start | bytes 7864324 | tf_op jit(solution)/shard_map/while
  229.0 5.6 %copy-start.6 = (bf16[2,256,40,64]{1,3,2,0:T(8,128)(2,1)S(1)}, bf16[2,256,40,64]{1,3,2,0:T(8,128)(2,1)}, u32[]{:S(2)}) copy-start(bf16[2,256,40,64]{1,3,2,0:T(8,128)(2,1)} %get-tuple-element.377) | copy-start | bytes 7864324 | tf_op jit(solution)/shard_map/while
  238.3 6.8 %copy-start.13 = (u32[256]{0:T(256)S(1)}, u32[256]{0:T(256)}, u32[]{:S(2)}) copy-start(u32[256]{0:T(256)} %constant.93) | copy-start | bytes 3076
  244.0 1.1 copy-start.2
  245.0 136.8 %all-reduce.3.cloned.1.call-start = ((), (), s32[]{:S(2)}) async-start(), calls=%async_computation | async-start | bytes 2621440 | tf_op jit(solution)/shard_map/psum | solution.py:31
  302.8 3.4 copy-start.3
  306.1 77.3 %copy-start.12 = (f32[40]{0:T(128)S(1)}, f32[40]{0:T(128)}, u32[]{:S(2)}) copy-start(f32[40]{0:T(128)} %param.25) | copy-start | bytes 484
  307.4 164.1 %all-gather.11.cloned.1.call-start = ((), (), s32[]{:S(2)}) async-start(), calls=%async_computation.2 | async-start | bytes 5406720 | tf_op jit(solution)/shard_map/all_gather | solution.py:142
  410.6 4.8 %copy-start.4 = (f32[512,2560]{1,0:T(8,128)S(1)}, f32[512,2560]{1,0:T(8,128)}, u32[]{:S(2)}) copy-start(f32[512,2560]{1,0:T(8,128)} %reshape.125) | copy-start | bytes 15728644
  410.6 4.8 %copy-start.11 = (f32[2560]{0:T(1024)S(1)}, f32[2560]{0:T(1024)}, u32[]{:S(2)}) copy-start(f32[2560]{0:T(1024)} %param.26) | copy-start | bytes 30724
  415.4 60.0 %copy-start.1 = (bf16[1,512,2560]{2,1,0:T(8,128)(2,1)S(1)}, bf16[1,512,2560]{2,1,0:T(8,128)(2,1)}, u32[]{:S(2)}) copy-start(bf16[1,512,2560]{2,1,0:T(8,128)(2,1)} %param.18) | copy-start | bytes 7864324
Sparse Core Ops, SparseCore 0:
  11.7 137.2 all-gather.12
  245.2 57.4 all-gather.8
  307.6 74.2 all-reduce.2
  384.9 86.6 all-gather.10
where the time goes:
time: 484 us; the launch traced here: 482 us
  waiting for transfers between devices  235 us (49%)
  blocking collectives  80.5 us (17%)
  local copies, waits for them, and re-layouts  72.7 us (15%)
  other arithmetic  39.5 us (8%)
  matrix products  35.3 us (7%)
  between operations  16 us (3%)
    psum x1, waiting for transfers between devices, broadcast(): return lax.psum(jnp.where(mine, x, jnp.zeros_like(x)), axis)  74.1 us
    all_gather x1, blocking collectives, on_device(): lax.all_gather(step_weight, ('req', 'seq'), axis=0, tiled=True)  70.5 us
    all_gather x1, waiting for transfers between devices, on_device(): lax.all_gather(mix_weight, ('req', 'seq'), axis=0, tiled=True)  60.2 us
    all_gather x1, waiting for transfers between devices, on_device(): piece = lax.all_gather(own_state, 'req', axis=0, tiled=True)  51.5 us
    all_gather x1, waiting for transfers between devices, carried_in(): gathered = jax.tree.map(lambda a: lax.all_gather(a, axis), part)  46 us
    unnamed x30, local copies, waits for them, and re-layouts  32 us
    reshape x2, local copies, waits for them, and re-layouts, on_device(): (inner_out + carried).reshape(span, heads, head_dim)  18.2 us
    dot_general x1, matrix products, on_device(): mixed = jnp.dot(rows, whole_mix, preferred_element_type=jnp.float32)  11.5 us
  transfers between devices with their start and end apart: 5, of which 5 were waited for; matrix products, arithmetic and copies ran while one was open for 10% of the time, Pallas kernels for 0%

commit v1 on v0

--- a/solution.py
+++ b/solution.py
@@ -58,7 +58,12 @@
     place = seq_index * span + jnp.arange(span, dtype=jnp.int32)
     valid = ((place >= start) & (place < start + length)).astype(jnp.float32)
     whole_mix, whole_step = (
-        lax.all_gather(mix_weight, ("req", "seq"), axis=0, tiled=True),
+        jnp.concatenate(
+            lax.all_to_all(
+                jnp.stack([mix_weight] * lax.axis_size(("req", "seq"))), ("req", "seq"), 0, 0
+            ),
+            axis=0,
+        ),
         lax.all_gather(step_weight, ("req", "seq"), axis=0, tiled=True),
     )
     mixed = jnp.dot(rows, whole_mix, preferred_element_type=jnp.float32)

time: 484 us -> 932 us (1.93)
  blocking collectives: 80.5 us -> 565 us
  waiting for transfers between devices: 235 us -> 177 us
  starting transfers between devices: 2.72 us -> 18.4 us
    all_gather x1, blocking collectives: 70.5 us -> 554 us  [on_device(): lax.all_gather(step_weight, ('req', 'seq'), axis=0, tiled=True)]
    all_gather x1 -> x0, waiting for transfers between devices: 60.2 us -> none  [on_device(): lax.all_gather(mix_weight, ('req', 'seq'), axis=0, tiled=True)]
    unnamed x30 -> x39, local copies, waits for them, and re-layouts: 32 us -> 6.72 us
    reshape x0 -> x1, local copies, waits for them, and re-layouts: none -> 25.3 us  [on_device(): jnp.concatenate(lax.all_to_all(jnp.stack([mix_weight] * lax.axis_size(('r...]
    all_to_all x0 -> x1, starting transfers between devices: none -> 15.6 us  [on_device(): lax.all_to_all(jnp.stack([mix_weight] * lax.axis_size(('req', 'seq'))), (...]
  transfers between devices with their start and end apart: 5 -> 5, of which waited for: 5 -> 4; matrix products, arithmetic and copies ran while one was open for 10% -> 5% of each run, Pallas kernels for 0% -> 0%
where the time goes in v1:
time: 932 us; the launch traced here: 930 us
  blocking collectives  565 us (61%)
  waiting for transfers between devices  177 us (19%)
  local copies, waits for them, and re-layouts  81.5 us (9%)
  other arithmetic  37.5 us (4%)
  matrix products  34.6 us (4%)
  starting transfers between devices  18.4 us (2%)
  between operations  16 us (2%)
    all_gather x1, blocking collectives, on_device(): lax.all_gather(step_weight, ('req', 'seq'), axis=0, tiled=True)  554 us
    psum x1, waiting for transfers between devices, broadcast(): return lax.psum(jnp.where(mine, x, jnp.zeros_like(x)), axis)  74.1 us
    all_gather x1, waiting for transfers between devices, on_device(): piece = lax.all_gather(own_state, 'req', axis=0, tiled=True)  51.6 us
    all_gather x1, waiting for transfers between devices, carried_in(): gathered = jax.tree.map(lambda a: lax.all_gather(a, axis), part)  46 us
    reshape x1, local copies, waits for them, and re-layouts, on_device(): jnp.concatenate(lax.all_to_all(jnp.stack([mix_weight] * lax.axis_size(('r...  25.3 us
  transfers between devices with their start and end apart: 5, of which 4 were waited for; matrix products, arithmetic and copies ran while one was open for 5% of the time, Pallas kernels for 0%

profile of v1, /device:TPU:2, one launch (start us, length us, event | category | flops | bytes accessed | tf_op | source)
XLA Modules:
  0.0 930.2 jit_solution(17147431103008415207)
XLA Ops:
  7.2 8.9 stack.2
  16.1 15.6 %all-to-all-start = ((bf16[256,10,2816]{2,1,0:T(8,128)(2,1)}), bf16[256,10,2816]{2,1,0:T(8,128)(2,1)}, u32[]{:S(2)}, u32[]{:S(2)}) async-start(bf16[256,10,2816]{2,1,0:T(8,128)(2,1)} %stack.2), calls=%async_computation | async-start | bytes 46137344 | tf_op jit(solution)/shard_map/all_to_all | solution.py:62
  31.8 554.5 %all-gather.3 = bf16[256,10,40]{2,1,0:T(8,128)(2,1)} all-gather(bf16[1,10,40]{2,1,0:T(8,128)(2,1)S(1)} %bitcast.156), channel_id=1, replica_groups=mesh['req'=32,'seq'=8] {'req','seq'}, dimensions={0}, use_global_device_ids=true | all-gather | bytes 205600 | tf_op jit(solution)/shard_map/all_gather | solution.py:67
  593.9 25.3 %reshape.111 = bf16[2560,2816]{1,0:T(8,128)(2,1)} reshape(bf16[256,10,2816]{2,1,0:T(8,128)(2,1)} %all-to-all-done) | data formatting | bytes 28835840 | tf_op jit(solution)/shard_map/reshape | solution.py:61
  619.2 11.5 %multiply_convert_fusion.6 = bf16[512,2816]{1,0:T(8,128)(2,1)S(1)} fusion(bf16[2560,2816]{1,0:T(8,128)(2,1)} %reshape.111, f32[512]{0:T(512)S(1)} %fusion.50, bf16[1,512,2560]{2,1,0:T(8,128)(2,1)S(1)} %copy-done), kind=kOutput, calls=%fused_computation.48 | convolution fusion | flops 7384858624 | bytes 19924992 | tf_op jit(solution)/shard_map/dot_general | solution.py:69
  635.0 5.3 collective-permute-done
  640.3 7.8 multiply_convert_fusion.5
  651.3 7.5 reshape.128
  658.9 6.4 copy.40
  667.1 17.0 %while.39 = (s32[]{:T(128)}, f32[2,256,40,64]{1,3,2,0:T(8,128)}, f32[2,256,40]{1,2,0:T(8,128)S(1)}, f32[2,40,64,128]{3,2,1,0:T(8,128)}, bf16[2,256,40,64]{1,3,2,...) while((s32[]{:T(128)}, f32[2,256,40,64]{1,3,2,0:T(8,128)}, ...), condition=%wide.region_6.7_spmd, body=%wide.region_3.6_spmd.sunk | while | flops 536604800 | bytes 18677688 | solution.py:112
  668.3 5.3 bitcast_dynamic-update-slice_fusion.4
  676.8 5.3 bitcast_dynamic-update-slice_fusion.4
  686.2 5.6 while.41
  694.3 10.3 %all-reduce = f32[320]{0:T(512)S(1)} all-reduce(f32[320]{0:T(512)S(1)} %get-tuple-element.232), channel_id=2, replica_groups=mesh['req'=32,'seq'=8] {'seq'}, use_global_device_ids=true, to_apply=%add | all-reduce | flops 320 | bytes 2560
  704.7 46.0 %all-gather.7.cloned.1.call-done = f32[320,64,128]{2,1,0:T(8,128)} async-done(((f32[40,64,128]{2,1,0:T(8,128)}), f32[320,64,128]{2,1,0:T(8,128)}) %all-gather.7.cloned.1.call-update) | async-done | bytes 10485776 | tf_op jit(solution)/shard_map/all_gather | solution.py:18
  750.8 3.3 while.40
  755.8 74.1 %all-reduce.3.cloned.1.call-done = f32[40,64,128]{2,1,0:T(8,128)} async-done(((f32[40,64,128]{2,1,0:T(8,128)}), f32[40,64,128]{2,1,0:T(8,128)}) %all-reduce.3.cloned.1.call-update) | async-done | bytes 1310736 | tf_op jit(solution)/shard_map/psum | solution.py:31
  832.4 8.0 multiply_add_fusion.1
  840.4 8.6 copy.47
  849.1 9.6 %reshape.129 = f32[512,2560]{1,0:T(8,128)} reshape(f32[2,256,40,64]{3,2,1,0:T(8,128)} %copy.47) | data formatting | bytes 10485760 | tf_op jit(solution)/shard_map/reshape | solution.py:136
  858.7 4.4 multiply_reduce_fusion
  863.5 4.7 fusion.30
  868.2 51.6 %all-gather.9.cloned.1.call-done = f32[160,64,128]{2,1,0:T(8,128)} async-done(((f32[5,64,128]{2,1,0:T(8,128)}), f32[160,64,128]{2,1,0:T(8,128)}) %all-gather.9.cloned.1.call-update) | async-done | bytes 5242896 | tf_op jit(solution)/shard_map/all_gather | solution.py:147
  919.8 3.9 select_reduce_fusion
  (117 shorter events, 39.3 us)
Async XLA Ops:
  7.2 585.8 %copy-start = (bf16[1,512,2560]{2,1,0:T(8,128)(2,1)S(1)}, bf16[1,512,2560]{2,1,0:T(8,128)(2,1)}, u32[]{:S(2)}) copy-start(bf16[1,512,2560]{2,1,0:T(8,128)(2,1)} %param.18) | copy-start | bytes 7864324
  16.1 15.7 %copy-start.12 = (bf16[10,40]{1,0:T(8,128)(2,1)S(1)}, bf16[10,40]{1,0:T(8,128)(2,1)}, u32[]{:S(2)}) copy-start(bf16[10,40]{1,0:T(8,128)(2,1)} %param.20) | copy-start | bytes 2404
  16.1 571.6 %copy-start.14 = (s32[32]{0:T(128)S(1)}, s32[32]{0:T(128)}, u32[]{:S(2)}) copy-start(s32[32]{0:T(128)} %param.29) | copy-start | bytes 388
  16.1 572.3 %copy-start.16 = (s32[32]{0:T(128)S(1)}, s32[32]{0:T(128)}, u32[]{:S(2)}) copy-start(s32[32]{0:T(128)} %param.28) | copy-start | bytes 388
  16.1 573.6 %copy-start.17 = (s32[32]{0:T(128)S(1)}, s32[32]{0:T(128)}, u32[]{:S(2)}) copy-start(s32[32]{0:T(128)} %param.27) | copy-start | bytes 388
  16.1 576.9 %copy-start.13 = (f32[40]{0:T(128)S(1)}, f32[40]{0:T(128)}, u32[]{:S(2)}) copy-start(f32[40]{0:T(128)} %param.23) | copy-start | bytes 484
  16.1 577.8 %all-to-all-start = ((bf16[256,10,2816]{2,1,0:T(8,128)(2,1)}), bf16[256,10,2816]{2,1,0:T(8,128)(2,1)}, u32[]{:S(2)}, u32[]{:S(2)}) async-start(bf16[256,10,2816]{2,1,0:T(8,128)(2,1)} %stack.2), calls=%async_computation | async-start | bytes 46137344 | tf_op jit(solution)/shard_map/all_to_all | solution.py:62
  31.7 719.0 %all-gather.7.cloned.1.call-start = ((), (), s32[]{:S(2)}) async-start(), calls=%async_computation.2 | async-start | bytes 11796480 | tf_op jit(solution)/shard_map/all_gather | solution.py:18
  619.2 15.6 %copy-start.8 = (f32[4,2816]{1,0:T(4,128)S(1)}, f32[4,2816]{1,0:T(4,128)}, u32[]{:S(2)}) copy-start(f32[4,2816]{1,0:T(4,128)} %param.21) | copy-start | bytes 135172
  619.2 21.1 %copy-start.10 = (f32[2816]{0:T(1024)S(1)}, f32[2816]{0:T(1024)}, u32[]{:S(2)}) copy-start(f32[2816]{0:T(1024)} %param.22) | copy-start | bytes 33796
  630.7 1.6 copy-start.7
  632.3 8.0 collective-permute-start
  648.1 1.5 copy-start.5
  658.9 8.2 copy-start.9
  668.3 5.6 copy-start.6
  676.8 5.6 copy-start.6
  686.2 6.8 copy-start.18
  692.9 137.0 %all-reduce.3.cloned.1.call-start = ((), (), s32[]{:S(2)}) async-start(), calls=%async_computation.1 | async-start | bytes 2621440 | tf_op jit(solution)/shard_map/psum | solution.py:31
  750.8 3.4 copy-start.3
  754.2 77.3 %copy-start.15 = (f32[40]{0:T(128)S(1)}, f32[40]{0:T(128)}, u32[]{:S(2)}) copy-start(f32[40]{0:T(128)} %param.25) | copy-start | bytes 484
  755.5 164.3 %all-gather.9.cloned.1.call-start = ((), (), s32[]{:S(2)}) async-start(), calls=%async_computation.3 | async-start | bytes 5406720 | tf_op jit(solution)/shard_map/all_gather | solution.py:147
  858.7 4.8 copy-start.4
  858.7 4.8 copy-start.11
  863.5 60.1 %copy-start.1 = (bf16[1,512,2560]{2,1,0:T(8,128)(2,1)S(1)}, bf16[1,512,2560]{2,1,0:T(8,128)(2,1)}, u32[]{:S(2)}) copy-start(bf16[1,512,2560]{2,1,0:T(8,128)(2,1)} %param.18) | copy-start | bytes 7864324
  (1 other events, 1.1 us)
Sparse Core Ops, SparseCore 0:
  693.0 57.6 all-gather.6
  755.6 74.2 all-reduce.2
  833.1 86.6 all-gather.8
